TPU v7x, 256 devices: a whole 4x4x8 slice. The times are simulated.
256 devices in a mesh: scan: 64 (over x, y_hi, z), tile: 4 (over y_lo, core).
Axes of the slice: x: 4, y: 4 (y_hi: 2, y_lo: 2; y = y_hi * 2 + y_lo), z: 8, core: 2. Of those that a mesh axis runs over, the one named last changes fastest.
Arguments:
- probe_modes: float32 [3072, 256], P(('scan', 'tile')), may hold values from -2.1 to 2.1
- object_tiles: float32 [4, 2, 2, 320, 320], P('tile'), may hold values from -4 to 4
- scan_offsets: int32 [512, 2], P(('scan', 'tile')), may hold values from 0 to 64, as said below
- patch_tiles: int32 [512], P(('scan', 'tile')), may hold values from 0 to 3, as said below
- amplitudes: bfloat16 [512, 256, 256], P(('scan', 'tile')), may hold values from 0.5 to 20
Outputs:
- probe_gradient: float32 [3072, 256], P(('scan', 'tile'))
- object_gradient: float32 [4, 2, 2, 320, 320], P('tile', None, None, 'scan')
Inputs may be any that keep to these rules, and one draw needn't show every extreme that they name: `patch_tiles`: each entry names the tile that wholly holds the patch of its position. `scan_offsets`: every patch lies wholly inside its tile.
All inputs are finite; a program needn't handle non-finite values.
Results may differ from a plain program's by a relative error of at most 0.02.
Values sent between devices are 32-bit elements; how exact they have to be, the bound alone decides.
No kernel may reach another device: no remote copies, remote signals or barrier semaphores. Data moves between devices by JAX's collectives and lax.ppermute only.
A program may use at most 128 MiB of HBM per device.

v0:
```python
import math
import jax
import jax.numpy as jnp
from jax import lax
from jax.sharding import PartitionSpec as P


def complex_tables(pixels):
    pixel_index = jnp.arange(pixels, dtype=jnp.int32)
    offset = pixel_index[:, None] - pixel_index[None, :]
    chirp_phase = (offset * offset % (2 * pixels)).astype(jnp.float32) * (math.pi / pixels)
    product = (pixel_index[:, None] * pixel_index[None, :] % pixels).astype(jnp.float32) * (
        2.0 * math.pi / pixels
    )
    norm_scale = 1.0 / math.sqrt(pixels)
    fresnel = (jnp.stack([jnp.cos(chirp_phase), jnp.sin(chirp_phase)]) * norm_scale).astype(
        jnp.bfloat16
    )
    spectral = (jnp.stack([jnp.cos(product), -jnp.sin(product)]) * norm_scale).astype(jnp.bfloat16)
    return (fresnel, spectral)


def multiply_object(exit_wave, object_patch):
    real_part = exit_wave[0] * object_patch[0] - exit_wave[1] * object_patch[1]
    imag_part = exit_wave[0] * object_patch[1] + exit_wave[1] * object_patch[0]
    return jnp.stack([real_part, imag_part])


def left_side(matrix_part, component):
    return jnp.einsum("ij,mjk->mik", matrix_part, component, preferred_element_type=jnp.float32)


def right_side(component, matrix_part):
    return jnp.einsum("mik,jk->mij", component, matrix_part, preferred_element_type=jnp.float32)


def left_product(matrix, exit_wave):
    real_part = left_side(matrix[0], exit_wave[0]) - left_side(matrix[1], exit_wave[1])
    imag_part = left_side(matrix[0], exit_wave[1]) + left_side(matrix[1], exit_wave[0])
    return jnp.stack([real_part, imag_part])


def right_product(exit_wave, matrix):
    real_part = right_side(exit_wave[0], matrix[0]) - right_side(exit_wave[1], matrix[1])
    imag_part = right_side(exit_wave[0], matrix[1]) + right_side(exit_wave[1], matrix[0])
    return jnp.stack([real_part, imag_part])


def position_loss(probe_values, patch_values, amplitude, fresnel, spectral):
    exit_wave = probe_values
    layers = patch_values.shape[0]
    for slice_index in range(layers):
        exit_wave = multiply_object(exit_wave, patch_values[slice_index])
        matrix = fresnel if slice_index < layers - 1 else spectral
        rounded = exit_wave.astype(jnp.bfloat16)
        halfway = left_product(matrix, rounded).astype(jnp.bfloat16)
        exit_wave = right_product(halfway, matrix)
    intensity = jnp.sum(exit_wave * exit_wave, axis=(0, 1))
    residue = jnp.sqrt(intensity + 1.0) - amplitude.astype(jnp.float32)
    return jnp.sum(residue * residue)


def body(probe_modes, object_tiles, scan_offsets, patch_tiles, amplitudes):
    tile_count = lax.axis_size("tile")
    scan_count = lax.axis_size("scan")
    pixels = probe_modes.shape[1]
    layers = object_tiles.shape[1]
    side = object_tiles.shape[3]
    whole_probe = lax.all_gather(probe_modes, ("scan", "tile"), axis=0, tiled=True)
    probe_field = whole_probe.reshape(2, -1, pixels, pixels)
    fresnel, spectral = complex_tables(pixels)
    whole_object = lax.all_gather(object_tiles, "tile", axis=0, tiled=True)

    def cut_own(tile_number, corner):
        anchor = (tile_number, jnp.int32(0), jnp.int32(0), corner[0], corner[1])
        return lax.dynamic_slice(whole_object, anchor, (1, layers, 2, pixels, pixels))[0]

    own_patches = jax.vmap(cut_own)(patch_tiles, scan_offsets)

    def one_position(probe_total, inputs):
        object_patch, amplitude = inputs

        def local_loss(probe_values, patch_values):
            return position_loss(probe_values, patch_values, amplitude, fresnel, spectral)

        misfit, pullback = jax.vjp(local_loss, probe_field, object_patch)
        probe_part, patch_part = pullback(jnp.ones_like(misfit))
        return (probe_total + probe_part, patch_part)

    probe_total, patch_gradients = lax.scan(
        one_position, jnp.zeros_like(probe_field), (own_patches, amplitudes)
    )

    def add_patch(object_total, inputs):
        gradient_piece, tile_number, corner = inputs
        anchor = (tile_number, jnp.int32(0), jnp.int32(0), corner[0], corner[1])
        current = lax.dynamic_slice(object_total, anchor, (1,) + gradient_piece.shape)
        return (
            lax.dynamic_update_slice(object_total, current + gradient_piece[None], anchor),
            None,
        )

    whole_shape = (tile_count,) + object_tiles.shape[1:]
    object_total, _ = lax.scan(
        add_patch, jnp.zeros(whole_shape, jnp.float32), (patch_gradients, patch_tiles, scan_offsets)
    )
    row_count = side // scan_count
    arranged = object_total.reshape(tile_count, layers, 2, scan_count, row_count, side)
    arranged = arranged.transpose(3, 0, 1, 2, 4, 5).reshape(
        scan_count * tile_count, layers, 2, row_count, side
    )
    object_gradient = lax.psum_scatter(arranged, ("scan", "tile"), scatter_dimension=0, tiled=True)
    probe_gradient = lax.psum_scatter(
        probe_total.reshape(-1, pixels), ("scan", "tile"), scatter_dimension=0, tiled=True
    )
    return (probe_gradient, object_gradient)


def solution(mesh):
    placed = (
        P(("scan", "tile"), None),
        P("tile", None, None, None, None),
        P(("scan", "tile"), None),
        P(("scan", "tile")),
        P(("scan", "tile"), None, None),
    )
    return jax.shard_map(
        body,
        mesh=mesh,
        in_specs=placed,
        out_specs=(P(("scan", "tile"), None), P("tile", None, None, "scan", None)),
        check_vma=False,
    )
```

profile of v0, /device:TPU:6, one launch (start us, length us, event | category | flops | bytes accessed | tf_op | source)
XLA Modules:
  0.0 2013.1 jit_solution(5033408186173666694)
XLA Ops:
  12.0 415.8 %all-gather.6.cloned.1.call-done = f32[256,12,256]{2,1,0:T(8,128)} async-done(((f32[1,12,256]{2,1,0:T(8,128)}), f32[256,12,256]{2,1,0:T(8,128)}) %all-gather.6.cloned.1.call-update) | async-done | bytes 3145744 | tf_op jit(solution)/shard_map/all_gather | solution.py:69
  427.8 4.6 reshape.226
  432.4 2.4 copy.160
  434.8 72.6 %all-gather.4.cloned.1.call-done = f32[4,2,2,320,320]{4,3,2,1,0:T(8,128)} async-done(((f32[1,2,2,320,320]{4,3,2,1,0:T(8,128)}), f32[4,2,2,320,320]{4,3,2,1,0:T(8,128)}) %all-gather.4.cloned.1.call-update) | async-done | bytes 6553616 | tf_op jit(solution)/shard_map/all_gather | solution.py:72
  507.3 10.7 while.25
  508.0 4.7 bitcast_dynamic-update-slice_fusion.4
  513.4 4.7 bitcast_dynamic-update-slice_fusion.4
  518.1 107.1 %while.26 = (s32[]{:T(128)}, f32[2,6,256,256]{2,3,1,0:T(8,128)}, f32[2,2,2,256,256]{4,3,2,1,0:T(8,128)}, f32[2,6,256,256]{2,3,1,0:T(8,128)S(1)}, f32[2,2,2,256,2...) while((s32[]{:T(128)}, f32[2,6,256,256]{2,3,1,0:T(8,128)}, ...), condition=%wide.region_10.11_spmd.clone, body=%wide.region_0.10_spmd.clone.sunk | while | flops 6493634560 | bytes 218235760 | solution.py:90
  518.4 3.0 dynamic-slice_bitcast_fusion.5
  545.6 3.6 fusion.382
  559.1 2.9 slice_multiply_fusion.9
  561.9 5.2 select_add_fusion.2
  567.2 3.0 dynamic-slice_bitcast_fusion.5
  594.3 3.6 fusion.382
  607.8 2.9 slice_multiply_fusion.9
  610.6 6.1 select_add_fusion.2
  625.2 5.7 broadcast_in_dim.99.clone
  630.9 202.0 %while.24 = (s32[]{:T(128)}, f32[4,2,2,320,320]{4,2,3,1,0:T(2,128)}, s32[2]{0:T(128)S(1)}, s32[2,2]{1,0:T(2,128)S(1)}, f32[2,2,2,256,256]{4,3,2,1,0:T(8,128)}, /*index=5*/s32[]{:T(128)}, s32[]{:T(128)}, s32[]{:T(128)}, s32[]{:T(128)}) while((s32[]{:T(128)}, f32[4,2,2,320,320]{4,2,3,1,0:T(2,128)}, s32[2]{0:T(128)S(1)}, ...), condition=%wide.region_13.14_spmd, body=%wide.region_12.13_spmd.sunk | while | flops 262155 | bytes 9437447 | solution.py:104
  637.9 2.6 constant_dynamic-slice_fusion.9
  642.7 89.2 %dynamic_update_slice.11 = f32[4,2,2,320,320]{4,2,3,1,0:T(2,128)} dynamic-update-slice(f32[4,2,2,320,320]{4,2,3,1,0:T(2,128)} %get-tuple-element.452, f32[1,2,2,256,256]{4,2,3,1,0:T(2,128)S(1)} %copy.201, s32[]{:T(128)S(6)} %select_n.91, s32[]{:T(128)} %constant.64.clone.1..sunk, s32[]{:T(128)} %constant.64.clone.1..sunk, s32[]{:T(128)S(6)} %select_n.92, s32[]{:T(128)S(6)} %select_n.93) | dynamic-update-slice | bytes 2097156 | tf_op jit(solution)/shard_map/while/body/eval_jaxpr/dynamic_update_slice | solution.py:99
  739.0 2.6 constant_dynamic-slice_fusion.9
  743.7 89.2 %dynamic_update_slice.11 = f32[4,2,2,320,320]{4,2,3,1,0:T(2,128)} dynamic-update-slice(f32[4,2,2,320,320]{4,2,3,1,0:T(2,128)} %get-tuple-element.452, f32[1,2,2,256,256]{4,2,3,1,0:T(2,128)S(1)} %copy.201, s32[]{:T(128)S(6)} %select_n.91, s32[]{:T(128)} %constant.64.clone.1..sunk, s32[]{:T(128)} %constant.64.clone.1..sunk, s32[]{:T(128)S(6)} %select_n.92, s32[]{:T(128)S(6)} %select_n.93) | dynamic-update-slice | bytes 2097156 | tf_op jit(solution)/shard_map/while/body/eval_jaxpr/dynamic_update_slice | solution.py:99
  833.0 9.0 copy.163
  843.9 2.3 copy.161
  846.2 592.8 %fusion = f32[16,256]{1,0:T(8,128)S(1)} fusion(f32[3072,256]{1,0:T(8,128)} %bitcast.555), kind=kCustom, calls=%all-reduce-scatter | all-reduce-scatter fusion | flops 1048577 | bytes 3162112
  1439.0 79.9 %collective-permute-start = (f32[16,256]{1,0:T(8,128)S(1)}, f32[16,256]{1,0:T(8,128)S(1)}, u32[]{:S(2)}, u32[]{:S(2)}) collective-permute-start(f32[16,256]{1,0:T(8,128)S(1)} %fusion), channel_id=1, source_target_pairs={{0,1},{1,2},{2,3},{3,4},{4,5},{5,6},{6,7},{7,8},{8,9},{9,10},{10,1... | collective-permute-start | bytes 49160
  1519.0 13.2 collective-permute-start.1
  1532.2 13.1 collective-permute-start.10
  1546.6 14.9 collective-permute-start.11
  1561.6 13.1 collective-permute-start.12
  1574.7 13.1 collective-permute-start.13
  1587.9 13.1 collective-permute-start.14
  1601.0 13.1 collective-permute-start.15
  1614.2 13.1 collective-permute-start.16
  1627.3 13.1 collective-permute-start.17
  1640.4 13.1 collective-permute-start.18
  1653.6 13.1 collective-permute-start.19
  1666.7 13.1 collective-permute-start.2
  1679.8 13.1 collective-permute-start.20
  1693.0 13.1 collective-permute-start.21
  1706.1 13.1 collective-permute-start.22
  1719.3 13.1 collective-permute-start.23
  1732.4 13.1 collective-permute-start.24
  1745.5 13.1 collective-permute-start.25
  1758.7 13.1 collective-permute-start.26
  1771.8 13.1 collective-permute-start.27
  1785.0 6.1 collective-permute-start.28
  1791.1 5.0 collective-permute-start.29
  1796.1 8.7 collective-permute-start.3
  1804.9 7.1 collective-permute-start.30
  1812.0 4.1 collective-permute-start.31
  1831.5 17.7 collective-permute-start.4
  1849.2 7.0 collective-permute-start.40
  1868.9 4.2 collective-permute-start.47
  1877.0 20.8 %collective-permute-start.5 = (f32[16,256]{1,0:T(8,128)S(1)}, f32[16,256]{1,0:T(8,128)S(1)}, u32[]{:S(2)}, u32[]{:S(2)}) collective-permute-start(f32[16,256]{1,0:T(8,128)S(1)} %fusion), channel_id=1, source_target_pairs={{0,6},{1,7},{2,8},{3,9},{4,10},{5,11},{6,12},{7,13},{8,14},{9,15},... | collective-permute-start | bytes 49160
  1897.8 10.3 collective-permute-start.50
  1912.0 2.1 collective-permute-start.53
  1925.8 13.3 collective-permute-start.6
  1939.1 8.0 collective-permute-start.60
  1951.0 9.8 collective-permute-start.7
  1960.7 13.1 collective-permute-start.8
  1973.9 13.1 collective-permute-start.9
  1987.0 10.1 collective-permute-done.9
  1997.1 7.2 concatenate.5
  (271 shorter events, 136.6 us)
Async XLA Ops:
  7.2 420.6 %all-gather.6.cloned.1.call-start = ((), (), s32[]{:S(2)}) async-start(), calls=%async_computation.1 | async-start | bytes 4210688 | tf_op jit(solution)/shard_map/all_gather | solution.py:69
  7.9 499.4 %all-gather.4.cloned.1.call-start = ((), (), s32[]{:S(2)}) async-start(), calls=%async_computation | async-start | bytes 9830400 | tf_op jit(solution)/shard_map/all_gather | solution.py:72
  8.7 1996.3 %all-reduce.39.cloned.1.call-start = ((), (), s32[]{:S(2)}) async-start(), calls=%async_computation.2 | async-start | bytes 15728640
  1439.0 135.7 %collective-permute-start = (f32[16,256]{1,0:T(8,128)S(1)}, f32[16,256]{1,0:T(8,128)S(1)}, u32[]{:S(2)}, u32[]{:S(2)}) collective-permute-start(f32[16,256]{1,0:T(8,128)S(1)} %fusion), channel_id=1, source_target_pairs={{0,1},{1,2},{2,3},{3,4},{4,5},{5,6},{6,7},{7,8},{8,9},{9,10},{10,1... | collective-permute-start | bytes 49160
  1519.0 68.9 %collective-permute-start.1 = (f32[16,256]{1,0:T(8,128)S(1)}, f32[16,256]{1,0:T(8,128)S(1)}, u32[]{:S(2)}, u32[]{:S(2)}) collective-permute-start(f32[16,256]{1,0:T(8,128)S(1)} %fusion), channel_id=1, source_target_pairs={{0,2},{1,3},{2,4},{3,5},{4,6},{5,7},{6,8},{7,9},{8,10},{9,11},{10,... | collective-permute-start | bytes 49160
  1532.2 68.8 %collective-permute-start.10 = (f32[16,256]{1,0:T(8,128)S(1)}, f32[16,256]{1,0:T(8,128)S(1)}, u32[]{:S(2)}, u32[]{:S(2)}) collective-permute-start(f32[16,256]{1,0:T(8,128)S(1)} %fusion), channel_id=1, source_target_pairs={{0,11},{1,12},{2,13},{3,14},{4,15},{5,16},{6,17},{7,18},{8,19},{9,... | collective-permute-start | bytes 49160
  1545.3 16.2 collective-permute-start.63
  1546.6 67.5 %collective-permute-start.11 = (f32[16,256]{1,0:T(8,128)S(1)}, f32[16,256]{1,0:T(8,128)S(1)}, u32[]{:S(2)}, u32[]{:S(2)}) collective-permute-start(f32[16,256]{1,0:T(8,128)S(1)} %fusion), channel_id=1, source_target_pairs={{0,12},{1,13},{2,14},{3,15},{4,16},{5,17},{6,18},{7,19},{8,20},{9,... | collective-permute-start | bytes 49160
  1561.6 65.7 %collective-permute-start.12 = (f32[16,256]{1,0:T(8,128)S(1)}, f32[16,256]{1,0:T(8,128)S(1)}, u32[]{:S(2)}, u32[]{:S(2)}) collective-permute-start(f32[16,256]{1,0:T(8,128)S(1)} %fusion), channel_id=1, source_target_pairs={{0,13},{1,14},{2,15},{3,16},{4,17},{5,18},{6,19},{7,20},{8,21},{9,... | collective-permute-start | bytes 49160
  1574.7 65.7 %collective-permute-start.13 = (f32[16,256]{1,0:T(8,128)S(1)}, f32[16,256]{1,0:T(8,128)S(1)}, u32[]{:S(2)}, u32[]{:S(2)}) collective-permute-start(f32[16,256]{1,0:T(8,128)S(1)} %fusion), channel_id=1, source_target_pairs={{0,14},{1,15},{2,16},{3,17},{4,18},{5,19},{6,20},{7,21},{8,22},{9,... | collective-permute-start | bytes 49160
  1587.9 65.7 %collective-permute-start.14 = (f32[16,256]{1,0:T(8,128)S(1)}, f32[16,256]{1,0:T(8,128)S(1)}, u32[]{:S(2)}, u32[]{:S(2)}) collective-permute-start(f32[16,256]{1,0:T(8,128)S(1)} %fusion), channel_id=1, source_target_pairs={{0,15},{1,16},{2,17},{3,18},{4,19},{5,20},{6,21},{7,22},{8,23},{9,... | collective-permute-start | bytes 49160
  1601.0 65.7 %collective-permute-start.15 = (f32[16,256]{1,0:T(8,128)S(1)}, f32[16,256]{1,0:T(8,128)S(1)}, u32[]{:S(2)}, u32[]{:S(2)}) collective-permute-start(f32[16,256]{1,0:T(8,128)S(1)} %fusion), channel_id=1, source_target_pairs={{0,16},{1,17},{2,18},{3,19},{4,20},{5,21},{6,22},{7,23},{8,24},{9,... | collective-permute-start | bytes 49160
  1614.2 65.7 %collective-permute-start.16 = (f32[16,256]{1,0:T(8,128)S(1)}, f32[16,256]{1,0:T(8,128)S(1)}, u32[]{:S(2)}, u32[]{:S(2)}) collective-permute-start(f32[16,256]{1,0:T(8,128)S(1)} %fusion), channel_id=1, source_target_pairs={{0,17},{1,18},{2,19},{3,20},{4,21},{5,22},{6,23},{7,24},{8,25},{9,... | collective-permute-start | bytes 49160
  1627.3 65.7 %collective-permute-start.17 = (f32[16,256]{1,0:T(8,128)S(1)}, f32[16,256]{1,0:T(8,128)S(1)}, u32[]{:S(2)}, u32[]{:S(2)}) collective-permute-start(f32[16,256]{1,0:T(8,128)S(1)} %fusion), channel_id=1, source_target_pairs={{0,18},{1,19},{2,20},{3,21},{4,22},{5,23},{6,24},{7,25},{8,26},{9,... | collective-permute-start | bytes 49160
  1640.4 65.7 %collective-permute-start.18 = (f32[16,256]{1,0:T(8,128)S(1)}, f32[16,256]{1,0:T(8,128)S(1)}, u32[]{:S(2)}, u32[]{:S(2)}) collective-permute-start(f32[16,256]{1,0:T(8,128)S(1)} %fusion), channel_id=1, source_target_pairs={{0,19},{1,20},{2,21},{3,22},{4,23},{5,24},{6,25},{7,26},{8,27},{9,... | collective-permute-start | bytes 49160
  1653.6 65.7 %collective-permute-start.19 = (f32[16,256]{1,0:T(8,128)S(1)}, f32[16,256]{1,0:T(8,128)S(1)}, u32[]{:S(2)}, u32[]{:S(2)}) collective-permute-start(f32[16,256]{1,0:T(8,128)S(1)} %fusion), channel_id=1, source_target_pairs={{0,20},{1,21},{2,22},{3,23},{4,24},{5,25},{6,26},{7,27},{8,28},{9,... | collective-permute-start | bytes 49160
  1666.7 65.7 %collective-permute-start.2 = (f32[16,256]{1,0:T(8,128)S(1)}, f32[16,256]{1,0:T(8,128)S(1)}, u32[]{:S(2)}, u32[]{:S(2)}) collective-permute-start(f32[16,256]{1,0:T(8,128)S(1)} %fusion), channel_id=1, source_target_pairs={{0,3},{1,4},{2,5},{3,6},{4,7},{5,8},{6,9},{7,10},{8,11},{9,12},{10... | collective-permute-start | bytes 49160
  1679.8 65.7 %collective-permute-start.20 = (f32[16,256]{1,0:T(8,128)S(1)}, f32[16,256]{1,0:T(8,128)S(1)}, u32[]{:S(2)}, u32[]{:S(2)}) collective-permute-start(f32[16,256]{1,0:T(8,128)S(1)} %fusion), channel_id=1, source_target_pairs={{0,21},{1,22},{2,23},{3,24},{4,25},{5,26},{6,27},{7,28},{8,29},{9,... | collective-permute-start | bytes 49160
  1693.0 65.7 %collective-permute-start.21 = (f32[16,256]{1,0:T(8,128)S(1)}, f32[16,256]{1,0:T(8,128)S(1)}, u32[]{:S(2)}, u32[]{:S(2)}) collective-permute-start(f32[16,256]{1,0:T(8,128)S(1)} %fusion), channel_id=1, source_target_pairs={{0,22},{1,23},{2,24},{3,25},{4,26},{5,27},{6,28},{7,29},{8,30},{9,... | collective-permute-start | bytes 49160
  1706.1 65.7 %collective-permute-start.22 = (f32[16,256]{1,0:T(8,128)S(1)}, f32[16,256]{1,0:T(8,128)S(1)}, u32[]{:S(2)}, u32[]{:S(2)}) collective-permute-start(f32[16,256]{1,0:T(8,128)S(1)} %fusion), channel_id=1, source_target_pairs={{0,23},{1,24},{2,25},{3,26},{4,27},{5,28},{6,29},{7,30},{8,31},{9,... | collective-permute-start | bytes 49160
  1719.3 65.7 %collective-permute-start.23 = (f32[16,256]{1,0:T(8,128)S(1)}, f32[16,256]{1,0:T(8,128)S(1)}, u32[]{:S(2)}, u32[]{:S(2)}) collective-permute-start(f32[16,256]{1,0:T(8,128)S(1)} %fusion), channel_id=1, source_target_pairs={{0,24},{1,25},{2,26},{3,27},{4,28},{5,29},{6,30},{7,31},{8,32},{9,... | collective-permute-start | bytes 49160
  1732.4 58.7 %collective-permute-start.24 = (f32[16,256]{1,0:T(8,128)S(1)}, f32[16,256]{1,0:T(8,128)S(1)}, u32[]{:S(2)}, u32[]{:S(2)}) collective-permute-start(f32[16,256]{1,0:T(8,128)S(1)} %fusion), channel_id=1, source_target_pairs={{0,25},{1,26},{2,27},{3,28},{4,29},{5,30},{6,31},{7,32},{8,33},{9,... | collective-permute-start | bytes 49160
  1745.5 50.6 %collective-permute-start.25 = (f32[16,256]{1,0:T(8,128)S(1)}, f32[16,256]{1,0:T(8,128)S(1)}, u32[]{:S(2)}, u32[]{:S(2)}) collective-permute-start(f32[16,256]{1,0:T(8,128)S(1)} %fusion), channel_id=1, source_target_pairs={{0,26},{1,27},{2,28},{3,29},{4,30},{5,31},{6,32},{7,33},{8,34},{9,... | collective-permute-start | bytes 49160
  1758.7 46.2 %collective-permute-start.26 = (f32[16,256]{1,0:T(8,128)S(1)}, f32[16,256]{1,0:T(8,128)S(1)}, u32[]{:S(2)}, u32[]{:S(2)}) collective-permute-start(f32[16,256]{1,0:T(8,128)S(1)} %fusion), channel_id=1, source_target_pairs={{0,27},{1,28},{2,29},{3,30},{4,31},{5,32},{6,33},{7,34},{8,35},{9,... | collective-permute-start | bytes 49160
  1771.8 40.1 %collective-permute-start.27 = (f32[16,256]{1,0:T(8,128)S(1)}, f32[16,256]{1,0:T(8,128)S(1)}, u32[]{:S(2)}, u32[]{:S(2)}) collective-permute-start(f32[16,256]{1,0:T(8,128)S(1)} %fusion), channel_id=1, source_target_pairs={{0,28},{1,29},{2,30},{3,31},{4,32},{5,33},{6,34},{7,35},{8,36},{9,... | collective-permute-start | bytes 49160
  1785.0 31.1 %collective-permute-start.28 = (f32[16,256]{1,0:T(8,128)S(1)}, f32[16,256]{1,0:T(8,128)S(1)}, u32[]{:S(2)}, u32[]{:S(2)}) collective-permute-start(f32[16,256]{1,0:T(8,128)S(1)} %fusion), channel_id=1, source_target_pairs={{0,29},{1,30},{2,31},{3,32},{4,33},{5,34},{6,35},{7,36},{8,37},{9,... | collective-permute-start | bytes 49160
  1791.1 26.9 %collective-permute-start.29 = (f32[16,256]{1,0:T(8,128)S(1)}, f32[16,256]{1,0:T(8,128)S(1)}, u32[]{:S(2)}, u32[]{:S(2)}) collective-permute-start(f32[16,256]{1,0:T(8,128)S(1)} %fusion), channel_id=1, source_target_pairs={{0,30},{1,31},{2,32},{3,33},{4,34},{5,35},{6,36},{7,37},{8,38},{9,... | collective-permute-start | bytes 49160
  1796.1 23.8 %collective-permute-start.3 = (f32[16,256]{1,0:T(8,128)S(1)}, f32[16,256]{1,0:T(8,128)S(1)}, u32[]{:S(2)}, u32[]{:S(2)}) collective-permute-start(f32[16,256]{1,0:T(8,128)S(1)} %fusion), channel_id=1, source_target_pairs={{0,4},{1,5},{2,6},{3,7},{4,8},{5,9},{6,10},{7,11},{8,12},{9,13},{1... | collective-permute-start | bytes 49160
  1804.9 17.0 collective-permute-start.30
  1812.0 11.8 collective-permute-start.31
  1816.0 9.7 collective-permute-start.32
  1818.0 9.7 collective-permute-start.33
  1819.9 9.7 collective-permute-start.34
  1823.8 25.4 %collective-permute-start.36 = (f32[16,256]{1,0:T(8,128)S(1)}, f32[16,256]{1,0:T(8,128)S(1)}, u32[]{:S(2)}, u32[]{:S(2)}) collective-permute-start(f32[16,256]{1,0:T(8,128)S(1)} %fusion), channel_id=1, source_target_pairs={{0,37},{1,38},{2,39},{3,40},{4,41},{5,42},{6,43},{7,44},{8,45},{9,... | collective-permute-start | bytes 49160
  1825.7 30.5 %collective-permute-start.37 = (f32[16,256]{1,0:T(8,128)S(1)}, f32[16,256]{1,0:T(8,128)S(1)}, u32[]{:S(2)}, u32[]{:S(2)}) collective-permute-start(f32[16,256]{1,0:T(8,128)S(1)} %fusion), channel_id=1, source_target_pairs={{0,38},{1,39},{2,40},{3,41},{4,42},{5,43},{6,44},{7,45},{8,46},{9,... | collective-permute-start | bytes 49160
  1827.7 30.5 %collective-permute-start.38 = (f32[16,256]{1,0:T(8,128)S(1)}, f32[16,256]{1,0:T(8,128)S(1)}, u32[]{:S(2)}, u32[]{:S(2)}) collective-permute-start(f32[16,256]{1,0:T(8,128)S(1)} %fusion), channel_id=1, source_target_pairs={{0,39},{1,40},{2,41},{3,42},{4,43},{5,44},{6,45},{7,46},{8,47},{9,... | collective-permute-start | bytes 49160
  1829.6 30.5 %collective-permute-start.39 = (f32[16,256]{1,0:T(8,128)S(1)}, f32[16,256]{1,0:T(8,128)S(1)}, u32[]{:S(2)}, u32[]{:S(2)}) collective-permute-start(f32[16,256]{1,0:T(8,128)S(1)} %fusion), channel_id=1, source_target_pairs={{0,40},{1,41},{2,42},{3,43},{4,44},{5,45},{6,46},{7,47},{8,48},{9,... | collective-permute-start | bytes 49160
  1831.5 30.5 %collective-permute-start.4 = (f32[16,256]{1,0:T(8,128)S(1)}, f32[16,256]{1,0:T(8,128)S(1)}, u32[]{:S(2)}, u32[]{:S(2)}) collective-permute-start(f32[16,256]{1,0:T(8,128)S(1)} %fusion), channel_id=1, source_target_pairs={{0,5},{1,6},{2,7},{3,8},{4,9},{5,10},{6,11},{7,12},{8,13},{9,14},{... | collective-permute-start | bytes 49160
  1849.2 14.7 collective-permute-start.40
  1856.2 10.7 collective-permute-start.41
  1858.2 10.7 collective-permute-start.42
  1860.1 13.0 collective-permute-start.43
  1862.0 13.0 collective-permute-start.44
  1864.0 13.0 collective-permute-start.45
  1866.9 30.9 %collective-permute-start.46 = (f32[16,256]{1,0:T(8,128)S(1)}, f32[16,256]{1,0:T(8,128)S(1)}, u32[]{:S(2)}, u32[]{:S(2)}) collective-permute-start(f32[16,256]{1,0:T(8,128)S(1)} %fusion), channel_id=1, source_target_pairs={{0,47},{1,48},{2,49},{3,50},{4,51},{5,52},{6,53},{7,54},{8,55},{9,... | collective-permute-start | bytes 49160
  1868.9 39.3 %collective-permute-start.47 = (f32[16,256]{1,0:T(8,128)S(1)}, f32[16,256]{1,0:T(8,128)S(1)}, u32[]{:S(2)}, u32[]{:S(2)}) collective-permute-start(f32[16,256]{1,0:T(8,128)S(1)} %fusion), channel_id=1, source_target_pairs={{0,48},{1,49},{2,50},{3,51},{4,52},{5,53},{6,54},{7,55},{8,56},{9,... | collective-permute-start | bytes 49160
  1873.1 36.9 %collective-permute-start.48 = (f32[16,256]{1,0:T(8,128)S(1)}, f32[16,256]{1,0:T(8,128)S(1)}, u32[]{:S(2)}, u32[]{:S(2)}) collective-permute-start(f32[16,256]{1,0:T(8,128)S(1)} %fusion), channel_id=1, source_target_pairs={{0,49},{1,50},{2,51},{3,52},{4,53},{5,54},{6,55},{7,56},{8,57},{9,... | collective-permute-start | bytes 49160
  1875.1 36.9 %collective-permute-start.49 = (f32[16,256]{1,0:T(8,128)S(1)}, f32[16,256]{1,0:T(8,128)S(1)}, u32[]{:S(2)}, u32[]{:S(2)}) collective-permute-start(f32[16,256]{1,0:T(8,128)S(1)} %fusion), channel_id=1, source_target_pairs={{0,50},{1,51},{2,52},{3,53},{4,54},{5,55},{6,56},{7,57},{8,58},{9,... | collective-permute-start | bytes 49160
  1877.0 37.1 %collective-permute-start.5 = (f32[16,256]{1,0:T(8,128)S(1)}, f32[16,256]{1,0:T(8,128)S(1)}, u32[]{:S(2)}, u32[]{:S(2)}) collective-permute-start(f32[16,256]{1,0:T(8,128)S(1)} %fusion), channel_id=1, source_target_pairs={{0,6},{1,7},{2,8},{3,9},{4,10},{5,11},{6,12},{7,13},{8,14},{9,15},... | collective-permute-start | bytes 49160
  1897.8 18.2 collective-permute-start.50
  1908.1 9.9 collective-permute-start.51
  1910.1 9.9 collective-permute-start.52
  1912.0 9.9 collective-permute-start.53
  1918.0 21.1 %collective-permute-start.56 = (f32[16,256]{1,0:T(8,128)S(1)}, f32[16,256]{1,0:T(8,128)S(1)}, u32[]{:S(2)}, u32[]{:S(2)}) collective-permute-start(f32[16,256]{1,0:T(8,128)S(1)} %fusion), channel_id=1, source_target_pairs={{0,57},{1,58},{2,59},{3,60},{4,61},{5,62},{6,63},{7,64},{8,65},{9,... | collective-permute-start | bytes 49160
  1920.0 27.1 %collective-permute-start.57 = (f32[16,256]{1,0:T(8,128)S(1)}, f32[16,256]{1,0:T(8,128)S(1)}, u32[]{:S(2)}, u32[]{:S(2)}) collective-permute-start(f32[16,256]{1,0:T(8,128)S(1)} %fusion), channel_id=1, source_target_pairs={{0,58},{1,59},{2,60},{3,61},{4,62},{5,63},{6,64},{7,65},{8,66},{9,... | collective-permute-start | bytes 49160
  1921.9 27.1 %collective-permute-start.58 = (f32[16,256]{1,0:T(8,128)S(1)}, f32[16,256]{1,0:T(8,128)S(1)}, u32[]{:S(2)}, u32[]{:S(2)}) collective-permute-start(f32[16,256]{1,0:T(8,128)S(1)} %fusion), channel_id=1, source_target_pairs={{0,59},{1,60},{2,61},{3,62},{4,63},{5,64},{6,65},{7,66},{8,67},{9,... | collective-permute-start | bytes 49160
  1923.8 27.1 %collective-permute-start.59 = (f32[16,256]{1,0:T(8,128)S(1)}, f32[16,256]{1,0:T(8,128)S(1)}, u32[]{:S(2)}, u32[]{:S(2)}) collective-permute-start(f32[16,256]{1,0:T(8,128)S(1)} %fusion), channel_id=1, source_target_pairs={{0,60},{1,61},{2,62},{3,63},{4,64},{5,65},{6,66},{7,67},{8,68},{9,... | collective-permute-start | bytes 49160
  1925.8 34.9 %collective-permute-start.6 = (f32[16,256]{1,0:T(8,128)S(1)}, f32[16,256]{1,0:T(8,128)S(1)}, u32[]{:S(2)}, u32[]{:S(2)}) collective-permute-start(f32[16,256]{1,0:T(8,128)S(1)} %fusion), channel_id=1, source_target_pairs={{0,7},{1,8},{2,9},{3,10},{4,11},{5,12},{6,13},{7,14},{8,15},{9,16}... | collective-permute-start | bytes 49160
  1939.1 34.8 %collective-permute-start.60 = (f32[16,256]{1,0:T(8,128)S(1)}, f32[16,256]{1,0:T(8,128)S(1)}, u32[]{:S(2)}, u32[]{:S(2)}) collective-permute-start(f32[16,256]{1,0:T(8,128)S(1)} %fusion), channel_id=1, source_target_pairs={{0,61},{1,62},{2,63},{3,64},{4,65},{5,66},{6,67},{7,68},{8,69},{9,... | collective-permute-start | bytes 49160
  1947.1 39.9 %collective-permute-start.61 = (f32[16,256]{1,0:T(8,128)S(1)}, f32[16,256]{1,0:T(8,128)S(1)}, u32[]{:S(2)}, u32[]{:S(2)}) collective-permute-start(f32[16,256]{1,0:T(8,128)S(1)} %fusion), channel_id=1, source_target_pairs={{0,62},{1,63},{2,64},{3,65},{4,66},{5,67},{6,68},{7,69},{8,70},{9,... | collective-permute-start | bytes 49160
  1949.0 38.0 %collective-permute-start.62 = (f32[16,256]{1,0:T(8,128)S(1)}, f32[16,256]{1,0:T(8,128)S(1)}, u32[]{:S(2)}, u32[]{:S(2)}) collective-permute-start(f32[16,256]{1,0:T(8,128)S(1)} %fusion), channel_id=1, source_target_pairs={{0,63},{1,64},{2,65},{3,66},{4,67},{5,68},{6,69},{7,70},{8,71},{9,... | collective-permute-start | bytes 49160
  1951.0 36.1 %collective-permute-start.7 = (f32[16,256]{1,0:T(8,128)S(1)}, f32[16,256]{1,0:T(8,128)S(1)}, u32[]{:S(2)}, u32[]{:S(2)}) collective-permute-start(f32[16,256]{1,0:T(8,128)S(1)} %fusion), channel_id=1, source_target_pairs={{0,8},{1,9},{2,10},{3,11},{4,12},{5,13},{6,14},{7,15},{8,16},{9,17... | collective-permute-start | bytes 49160
  1960.7 26.3 %collective-permute-start.8 = (f32[16,256]{1,0:T(8,128)S(1)}, f32[16,256]{1,0:T(8,128)S(1)}, u32[]{:S(2)}, u32[]{:S(2)}) collective-permute-start(f32[16,256]{1,0:T(8,128)S(1)} %fusion), channel_id=1, source_target_pairs={{0,9},{1,10},{2,11},{3,12},{4,13},{5,14},{6,15},{7,16},{8,17},{9,1... | collective-permute-start | bytes 49160
  1973.9 23.3 %collective-permute-start.9 = (f32[16,256]{1,0:T(8,128)S(1)}, f32[16,256]{1,0:T(8,128)S(1)}, u32[]{:S(2)}, u32[]{:S(2)}) collective-permute-start(f32[16,256]{1,0:T(8,128)S(1)} %fusion), channel_id=1, source_target_pairs={{0,10},{1,11},{2,12},{3,13},{4,14},{5,15},{6,16},{7,17},{8,18},{9,... | collective-permute-start | bytes 49160
  (24 other events, 84.9 us)
Sparse Core Ops, SparseCore 0:
  9.9 417.8 all-gather.5
  429.6 77.6 all-gather.3
  842.1 281.0 all-reduce.38
where the time goes:
time: 2020 us; the launch traced here: 2010 us
  blocking collectives  593 us (29%)
  starting transfers between devices  546 us (27%)
  waiting for transfers between devices  501 us (25%)
  local copies, waits for them, and re-layouts  264 us (13%)
  other arithmetic  47 us (2%)
  matrix products  26.4 us (1%)
  loops' own time  21.1 us (1%)
    unnamed x1, blocking collectives  593 us
    unnamed x65, starting transfers between devices  546 us
    all_gather x1, waiting for transfers between devices, body(): lax.all_gather(probe_modes, ('scan', 'tile'), axis=0, tiled=True)  416 us
    dynamic_update_slice x4, local copies, waits for them, and re-layouts, add_patch(): lax.dynamic_update_slice(object_total, current + gradient_piece[None], an...  180 us
    all_gather x1, waiting for transfers between devices, body(): whole_object = lax.all_gather(object_tiles, 'tile', axis=0, tiled=True)  72.6 us
  transfers between devices with their start and end apart: 67, of which 4 were waited for; matrix products, arithmetic and copies ran while one was open for 30% of the time, Pallas kernels for 0%

commit v1 on v0

--- a/solution.py
+++ b/solution.py
@@ -66,7 +66,10 @@
     pixels = probe_modes.shape[1]
     layers = object_tiles.shape[1]
     side = object_tiles.shape[3]
-    whole_probe = lax.all_gather(probe_modes, ("scan", "tile"), axis=0, tiled=True)
+    size = lax.axis_size(("scan", "tile"))
+    tiles = jnp.stack([probe_modes for _ in range(size)])
+    tiles = lax.all_to_all(tiles, ("scan", "tile"), split_axis=0, concat_axis=0)
+    whole_probe = jnp.concatenate(tiles, axis=0)
     probe_field = whole_probe.reshape(2, -1, pixels, pixels)
     fresnel, spectral = complex_tables(pixels)
     whole_object = lax.all_gather(object_tiles, "tile", axis=0, tiled=True)

time: 2020 us -> 1650 us (0.82)
  waiting for transfers between devices: 501 us -> 110 us
    all_gather x1 -> x0, waiting for transfers between devices: 416 us -> none  [body(): lax.all_gather(probe_modes, ('scan', 'tile'), axis=0, tiled=True)]
    all_to_all x0 -> x1, waiting for transfers between devices: none -> 92.4 us  [body(): tiles = lax.all_to_all(tiles, ('scan', 'tile'), split_axis=0, concat_axis=0)]
    all_gather x1, waiting for transfers between devices: 72.6 us -> 5.89 us  [body(): whole_object = lax.all_gather(object_tiles, 'tile', axis=0, tiled=True)]
  transfers between devices with their start and end apart: 67 -> 67, of which waited for: 4 -> 4; matrix products, arithmetic and copies ran while one was open for 30% -> 38% of each run, Pallas kernels for 0% -> 0%
where the time goes in v1:
time: 1650 us; the launch traced here: 1640 us
  blocking collectives  592 us (36%)
  starting transfers between devices  562 us (34%)
  local copies, waits for them, and re-layouts  266 us (16%)
  waiting for transfers between devices  110 us (7%)
  other arithmetic  47.2 us (3%)
  matrix products  26.4 us (2%)
  loops' own time  21.1 us (1%)
    unnamed x1, blocking collectives  592 us
    unnamed x65, starting transfers between devices  546 us
    dynamic_update_slice x4, local copies, waits for them, and re-layouts, add_patch(): lax.dynamic_update_slice(object_total, current + gradient_piece[None], an...  180 us
    all_to_all x1, waiting for transfers between devices, body(): tiles = lax.all_to_all(tiles, ('scan', 'tile'), split_axis=0, concat_axis=0)  92.4 us
  transfers between devices with their start and end apart: 67, of which 4 were waited for; matrix products, arithmetic and copies ran while one was open for 38% of the time, Pallas kernels for 0%

profile of v1, /device:TPU:6, one launch (start us, length us, event | category | flops | bytes accessed | tf_op | source)
XLA Modules:
  0.0 1640.0 jit_solution(7232989515708015356)
XLA Ops:
  7.9 2.5 stack.22
  10.4 15.6 all-to-all-start
  29.4 92.4 %all-to-all-done = f32[256,12,256]{2,1,0:T(8,128)} async-done(((f32[256,12,256]{2,1,0:T(8,128)}), f32[256,12,256]{2,1,0:T(8,128)}, u32[]{:S(2)}, u32[]{:S(2)}) %all-to-all-start) | async-done | bytes 3145760 | tf_op jit(solution)/shard_map/all_to_all | solution.py:71
  121.8 4.6 reshape_reshape.3
  126.4 2.4 copy.160
  128.8 5.9 all-gather.2.cloned.1.call-done
  134.7 10.6 while.25
  135.3 4.7 bitcast_dynamic-update-slice_fusion.4
  140.7 4.6 bitcast_dynamic-update-slice_fusion.4
  145.3 107.2 %while.26 = (s32[]{:T(128)}, f32[2,6,256,256]{2,3,1,0:T(8,128)}, f32[2,2,2,256,256]{4,3,2,1,0:T(8,128)}, f32[2,6,256,256]{2,3,1,0:T(8,128)S(1)}, f32[2,2,2,256,2...) while((s32[]{:T(128)}, f32[2,6,256,256]{2,3,1,0:T(8,128)}, ...), condition=%wide.region_10.11_spmd.clone, body=%wide.region_0.10_spmd.clone.sunk | while | flops 6493634560 | bytes 218235760 | solution.py:93
  145.6 3.0 dynamic-slice_bitcast_fusion.5
  172.8 3.6 fusion.382
  186.2 2.9 slice_multiply_fusion.9
  189.2 5.3 select_add_fusion.2
  194.4 2.9 dynamic-slice_bitcast_fusion.5
  221.5 3.6 fusion.382
  235.0 2.9 slice_multiply_fusion.9
  237.9 6.1 select_add_fusion.2
  252.5 5.6 broadcast_in_dim.99.clone
  258.1 202.0 %while.24 = (s32[]{:T(128)}, f32[4,2,2,320,320]{4,2,3,1,0:T(2,128)}, s32[2]{0:T(128)S(1)}, s32[2,2]{1,0:T(2,128)S(1)}, f32[2,2,2,256,256]{4,3,2,1,0:T(8,128)}, /*index=5*/s32[]{:T(128)}, s32[]{:T(128)}, s32[]{:T(128)}, s32[]{:T(128)}) while((s32[]{:T(128)}, f32[4,2,2,320,320]{4,2,3,1,0:T(2,128)}, s32[2]{0:T(128)S(1)}, ...), condition=%wide.region_13.14_spmd, body=%wide.region_12.13_spmd.sunk | while | flops 262155 | bytes 9437447 | solution.py:107
  265.1 2.6 constant_dynamic-slice_fusion.9
  269.9 89.2 %dynamic_update_slice.11 = f32[4,2,2,320,320]{4,2,3,1,0:T(2,128)} dynamic-update-slice(f32[4,2,2,320,320]{4,2,3,1,0:T(2,128)} %get-tuple-element.452, f32[1,2,2,256,256]{4,2,3,1,0:T(2,128)S(1)} %copy.201, s32[]{:T(128)S(6)} %select_n.91, s32[]{:T(128)} %constant.64.clone.1..sunk, s32[]{:T(128)} %constant.64.clone.1..sunk, s32[]{:T(128)S(6)} %select_n.92, s32[]{:T(128)S(6)} %select_n.93) | dynamic-update-slice | bytes 2097156 | tf_op jit(solution)/shard_map/while/body/eval_jaxpr/dynamic_update_slice | solution.py:102
  366.2 2.6 constant_dynamic-slice_fusion.9
  370.9 89.3 %dynamic_update_slice.11 = f32[4,2,2,320,320]{4,2,3,1,0:T(2,128)} dynamic-update-slice(f32[4,2,2,320,320]{4,2,3,1,0:T(2,128)} %get-tuple-element.452, f32[1,2,2,256,256]{4,2,3,1,0:T(2,128)S(1)} %copy.201, s32[]{:T(128)S(6)} %select_n.91, s32[]{:T(128)} %constant.64.clone.1..sunk, s32[]{:T(128)} %constant.64.clone.1..sunk, s32[]{:T(128)S(6)} %select_n.92, s32[]{:T(128)S(6)} %select_n.93) | dynamic-update-slice | bytes 2097156 | tf_op jit(solution)/shard_map/while/body/eval_jaxpr/dynamic_update_slice | solution.py:102
  460.2 9.0 copy.163
  473.4 592.2 %fusion = f32[16,256]{1,0:T(8,128)S(1)} fusion(f32[3072,256]{1,0:T(8,128)} %bitcast.554), kind=kCustom, calls=%all-reduce-scatter | all-reduce-scatter fusion | flops 1048577 | bytes 3162112
  1065.6 79.9 %collective-permute-start = (f32[16,256]{1,0:T(8,128)S(1)}, f32[16,256]{1,0:T(8,128)S(1)}, u32[]{:S(2)}, u32[]{:S(2)}) collective-permute-start(f32[16,256]{1,0:T(8,128)S(1)} %fusion), channel_id=1, source_target_pairs={{0,1},{1,2},{2,3},{3,4},{4,5},{5,6},{6,7},{7,8},{8,9},{9,10},{10,1... | collective-permute-start | bytes 49160
  1145.6 13.2 collective-permute-start.1
  1158.8 13.1 collective-permute-start.10
  1173.3 14.9 collective-permute-start.11
  1188.2 13.1 collective-permute-start.12
  1201.3 13.1 collective-permute-start.13
  1214.5 13.1 collective-permute-start.14
  1227.6 13.1 collective-permute-start.15
  1240.8 13.1 collective-permute-start.16
  1253.9 13.1 collective-permute-start.17
  1267.0 13.1 collective-permute-start.18
  1280.2 13.1 collective-permute-start.19
  1293.3 13.1 collective-permute-start.2
  1306.5 13.1 collective-permute-start.20
  1319.6 13.1 collective-permute-start.21
  1332.7 13.1 collective-permute-start.22
  1345.9 13.1 collective-permute-start.23
  1359.0 13.1 collective-permute-start.24
  1372.2 13.1 collective-permute-start.25
  1385.3 13.1 collective-permute-start.26
  1398.4 13.1 collective-permute-start.27
  1411.6 6.1 collective-permute-start.28
  1417.7 5.0 collective-permute-start.29
  1422.8 8.7 collective-permute-start.3
  1431.5 7.1 collective-permute-start.30
  1438.6 4.1 collective-permute-start.31
  1458.2 17.7 %collective-permute-start.4 = (f32[16,256]{1,0:T(8,128)S(1)}, f32[16,256]{1,0:T(8,128)S(1)}, u32[]{:S(2)}, u32[]{:S(2)}) collective-permute-start(f32[16,256]{1,0:T(8,128)S(1)} %fusion), channel_id=1, source_target_pairs={{0,5},{1,6},{2,7},{3,8},{4,9},{5,10},{6,11},{7,12},{8,13},{9,14},{... | collective-permute-start | bytes 49160
  1475.8 7.0 collective-permute-start.40
  1495.5 4.2 collective-permute-start.47
  1503.6 20.8 %collective-permute-start.5 = (f32[16,256]{1,0:T(8,128)S(1)}, f32[16,256]{1,0:T(8,128)S(1)}, u32[]{:S(2)}, u32[]{:S(2)}) collective-permute-start(f32[16,256]{1,0:T(8,128)S(1)} %fusion), channel_id=1, source_target_pairs={{0,6},{1,7},{2,8},{3,9},{4,10},{5,11},{6,12},{7,13},{8,14},{9,15},... | collective-permute-start | bytes 49160
  1524.4 10.3 collective-permute-start.50
  1552.4 13.3 collective-permute-start.6
  1565.7 8.0 collective-permute-start.60
  1577.6 9.8 collective-permute-start.7
  1587.3 13.1 collective-permute-start.8
  1600.5 13.1 collective-permute-start.9
  1613.7 10.1 collective-permute-done.9
  1623.7 7.2 concatenate.5
  (273 shorter events, 140.3 us)
Async XLA Ops:
  7.2 127.5 %all-gather.2.cloned.1.call-start = ((), (), s32[]{:S(2)}) async-start(), calls=%async_computation.1 | async-start | bytes 9830400 | tf_op jit(solution)/shard_map/all_gather | solution.py:75
  10.4 111.4 %all-to-all-start = ((f32[256,12,256]{2,1,0:T(8,128)}), f32[256,12,256]{2,1,0:T(8,128)}, u32[]{:S(2)}, u32[]{:S(2)}) async-start(f32[256,12,256]{2,1,0:T(8,128)} %stack.22), calls=%async_computation | async-start | bytes 8388608 | tf_op jit(solution)/shard_map/all_to_all | solution.py:71
  26.0 1605.6 %all-reduce.39.cloned.1.call-start = ((), (), s32[]{:S(2)}) async-start(), calls=%async_computation.2 | async-start | bytes 15728640
  1065.6 135.7 %collective-permute-start = (f32[16,256]{1,0:T(8,128)S(1)}, f32[16,256]{1,0:T(8,128)S(1)}, u32[]{:S(2)}, u32[]{:S(2)}) collective-permute-start(f32[16,256]{1,0:T(8,128)S(1)} %fusion), channel_id=1, source_target_pairs={{0,1},{1,2},{2,3},{3,4},{4,5},{5,6},{6,7},{7,8},{8,9},{9,10},{10,1... | collective-permute-start | bytes 49160
  1145.6 68.9 %collective-permute-start.1 = (f32[16,256]{1,0:T(8,128)S(1)}, f32[16,256]{1,0:T(8,128)S(1)}, u32[]{:S(2)}, u32[]{:S(2)}) collective-permute-start(f32[16,256]{1,0:T(8,128)S(1)} %fusion), channel_id=1, source_target_pairs={{0,2},{1,3},{2,4},{3,5},{4,6},{5,7},{6,8},{7,9},{8,10},{9,11},{10,... | collective-permute-start | bytes 49160
  1158.8 68.8 %collective-permute-start.10 = (f32[16,256]{1,0:T(8,128)S(1)}, f32[16,256]{1,0:T(8,128)S(1)}, u32[]{:S(2)}, u32[]{:S(2)}) collective-permute-start(f32[16,256]{1,0:T(8,128)S(1)} %fusion), channel_id=1, source_target_pairs={{0,11},{1,12},{2,13},{3,14},{4,15},{5,16},{6,17},{7,18},{8,19},{9,... | collective-permute-start | bytes 49160
  1172.0 16.2 collective-permute-start.63
  1173.3 67.5 %collective-permute-start.11 = (f32[16,256]{1,0:T(8,128)S(1)}, f32[16,256]{1,0:T(8,128)S(1)}, u32[]{:S(2)}, u32[]{:S(2)}) collective-permute-start(f32[16,256]{1,0:T(8,128)S(1)} %fusion), channel_id=1, source_target_pairs={{0,12},{1,13},{2,14},{3,15},{4,16},{5,17},{6,18},{7,19},{8,20},{9,... | collective-permute-start | bytes 49160
  1188.2 65.7 %collective-permute-start.12 = (f32[16,256]{1,0:T(8,128)S(1)}, f32[16,256]{1,0:T(8,128)S(1)}, u32[]{:S(2)}, u32[]{:S(2)}) collective-permute-start(f32[16,256]{1,0:T(8,128)S(1)} %fusion), channel_id=1, source_target_pairs={{0,13},{1,14},{2,15},{3,16},{4,17},{5,18},{6,19},{7,20},{8,21},{9,... | collective-permute-start | bytes 49160
  1201.3 65.7 %collective-permute-start.13 = (f32[16,256]{1,0:T(8,128)S(1)}, f32[16,256]{1,0:T(8,128)S(1)}, u32[]{:S(2)}, u32[]{:S(2)}) collective-permute-start(f32[16,256]{1,0:T(8,128)S(1)} %fusion), channel_id=1, source_target_pairs={{0,14},{1,15},{2,16},{3,17},{4,18},{5,19},{6,20},{7,21},{8,22},{9,... | collective-permute-start | bytes 49160
  1214.5 65.7 %collective-permute-start.14 = (f32[16,256]{1,0:T(8,128)S(1)}, f32[16,256]{1,0:T(8,128)S(1)}, u32[]{:S(2)}, u32[]{:S(2)}) collective-permute-start(f32[16,256]{1,0:T(8,128)S(1)} %fusion), channel_id=1, source_target_pairs={{0,15},{1,16},{2,17},{3,18},{4,19},{5,20},{6,21},{7,22},{8,23},{9,... | collective-permute-start | bytes 49160
  1227.6 65.7 %collective-permute-start.15 = (f32[16,256]{1,0:T(8,128)S(1)}, f32[16,256]{1,0:T(8,128)S(1)}, u32[]{:S(2)}, u32[]{:S(2)}) collective-permute-start(f32[16,256]{1,0:T(8,128)S(1)} %fusion), channel_id=1, source_target_pairs={{0,16},{1,17},{2,18},{3,19},{4,20},{5,21},{6,22},{7,23},{8,24},{9,... | collective-permute-start | bytes 49160
  1240.8 65.7 %collective-permute-start.16 = (f32[16,256]{1,0:T(8,128)S(1)}, f32[16,256]{1,0:T(8,128)S(1)}, u32[]{:S(2)}, u32[]{:S(2)}) collective-permute-start(f32[16,256]{1,0:T(8,128)S(1)} %fusion), channel_id=1, source_target_pairs={{0,17},{1,18},{2,19},{3,20},{4,21},{5,22},{6,23},{7,24},{8,25},{9,... | collective-permute-start | bytes 49160
  1253.9 65.7 %collective-permute-start.17 = (f32[16,256]{1,0:T(8,128)S(1)}, f32[16,256]{1,0:T(8,128)S(1)}, u32[]{:S(2)}, u32[]{:S(2)}) collective-permute-start(f32[16,256]{1,0:T(8,128)S(1)} %fusion), channel_id=1, source_target_pairs={{0,18},{1,19},{2,20},{3,21},{4,22},{5,23},{6,24},{7,25},{8,26},{9,... | collective-permute-start | bytes 49160
  1267.0 65.7 %collective-permute-start.18 = (f32[16,256]{1,0:T(8,128)S(1)}, f32[16,256]{1,0:T(8,128)S(1)}, u32[]{:S(2)}, u32[]{:S(2)}) collective-permute-start(f32[16,256]{1,0:T(8,128)S(1)} %fusion), channel_id=1, source_target_pairs={{0,19},{1,20},{2,21},{3,22},{4,23},{5,24},{6,25},{7,26},{8,27},{9,... | collective-permute-start | bytes 49160
  1280.2 65.7 %collective-permute-start.19 = (f32[16,256]{1,0:T(8,128)S(1)}, f32[16,256]{1,0:T(8,128)S(1)}, u32[]{:S(2)}, u32[]{:S(2)}) collective-permute-start(f32[16,256]{1,0:T(8,128)S(1)} %fusion), channel_id=1, source_target_pairs={{0,20},{1,21},{2,22},{3,23},{4,24},{5,25},{6,26},{7,27},{8,28},{9,... | collective-permute-start | bytes 49160
  1293.3 65.7 %collective-permute-start.2 = (f32[16,256]{1,0:T(8,128)S(1)}, f32[16,256]{1,0:T(8,128)S(1)}, u32[]{:S(2)}, u32[]{:S(2)}) collective-permute-start(f32[16,256]{1,0:T(8,128)S(1)} %fusion), channel_id=1, source_target_pairs={{0,3},{1,4},{2,5},{3,6},{4,7},{5,8},{6,9},{7,10},{8,11},{9,12},{10... | collective-permute-start | bytes 49160
  1306.5 65.7 %collective-permute-start.20 = (f32[16,256]{1,0:T(8,128)S(1)}, f32[16,256]{1,0:T(8,128)S(1)}, u32[]{:S(2)}, u32[]{:S(2)}) collective-permute-start(f32[16,256]{1,0:T(8,128)S(1)} %fusion), channel_id=1, source_target_pairs={{0,21},{1,22},{2,23},{3,24},{4,25},{5,26},{6,27},{7,28},{8,29},{9,... | collective-permute-start | bytes 49160
  1319.6 65.7 %collective-permute-start.21 = (f32[16,256]{1,0:T(8,128)S(1)}, f32[16,256]{1,0:T(8,128)S(1)}, u32[]{:S(2)}, u32[]{:S(2)}) collective-permute-start(f32[16,256]{1,0:T(8,128)S(1)} %fusion), channel_id=1, source_target_pairs={{0,22},{1,23},{2,24},{3,25},{4,26},{5,27},{6,28},{7,29},{8,30},{9,... | collective-permute-start | bytes 49160
  1332.7 65.7 %collective-permute-start.22 = (f32[16,256]{1,0:T(8,128)S(1)}, f32[16,256]{1,0:T(8,128)S(1)}, u32[]{:S(2)}, u32[]{:S(2)}) collective-permute-start(f32[16,256]{1,0:T(8,128)S(1)} %fusion), channel_id=1, source_target_pairs={{0,23},{1,24},{2,25},{3,26},{4,27},{5,28},{6,29},{7,30},{8,31},{9,... | collective-permute-start | bytes 49160
  1345.9 65.7 %collective-permute-start.23 = (f32[16,256]{1,0:T(8,128)S(1)}, f32[16,256]{1,0:T(8,128)S(1)}, u32[]{:S(2)}, u32[]{:S(2)}) collective-permute-start(f32[16,256]{1,0:T(8,128)S(1)} %fusion), channel_id=1, source_target_pairs={{0,24},{1,25},{2,26},{3,27},{4,28},{5,29},{6,30},{7,31},{8,32},{9,... | collective-permute-start | bytes 49160
  1359.0 58.7 %collective-permute-start.24 = (f32[16,256]{1,0:T(8,128)S(1)}, f32[16,256]{1,0:T(8,128)S(1)}, u32[]{:S(2)}, u32[]{:S(2)}) collective-permute-start(f32[16,256]{1,0:T(8,128)S(1)} %fusion), channel_id=1, source_target_pairs={{0,25},{1,26},{2,27},{3,28},{4,29},{5,30},{6,31},{7,32},{8,33},{9,... | collective-permute-start | bytes 49160
  1372.2 50.6 %collective-permute-start.25 = (f32[16,256]{1,0:T(8,128)S(1)}, f32[16,256]{1,0:T(8,128)S(1)}, u32[]{:S(2)}, u32[]{:S(2)}) collective-permute-start(f32[16,256]{1,0:T(8,128)S(1)} %fusion), channel_id=1, source_target_pairs={{0,26},{1,27},{2,28},{3,29},{4,30},{5,31},{6,32},{7,33},{8,34},{9,... | collective-permute-start | bytes 49160
  1385.3 46.2 %collective-permute-start.26 = (f32[16,256]{1,0:T(8,128)S(1)}, f32[16,256]{1,0:T(8,128)S(1)}, u32[]{:S(2)}, u32[]{:S(2)}) collective-permute-start(f32[16,256]{1,0:T(8,128)S(1)} %fusion), channel_id=1, source_target_pairs={{0,27},{1,28},{2,29},{3,30},{4,31},{5,32},{6,33},{7,34},{8,35},{9,... | collective-permute-start | bytes 49160
  1398.4 40.1 %collective-permute-start.27 = (f32[16,256]{1,0:T(8,128)S(1)}, f32[16,256]{1,0:T(8,128)S(1)}, u32[]{:S(2)}, u32[]{:S(2)}) collective-permute-start(f32[16,256]{1,0:T(8,128)S(1)} %fusion), channel_id=1, source_target_pairs={{0,28},{1,29},{2,30},{3,31},{4,32},{5,33},{6,34},{7,35},{8,36},{9,... | collective-permute-start | bytes 49160
  1411.6 31.1 %collective-permute-start.28 = (f32[16,256]{1,0:T(8,128)S(1)}, f32[16,256]{1,0:T(8,128)S(1)}, u32[]{:S(2)}, u32[]{:S(2)}) collective-permute-start(f32[16,256]{1,0:T(8,128)S(1)} %fusion), channel_id=1, source_target_pairs={{0,29},{1,30},{2,31},{3,32},{4,33},{5,34},{6,35},{7,36},{8,37},{9,... | collective-permute-start | bytes 49160
  1417.7 26.9 %collective-permute-start.29 = (f32[16,256]{1,0:T(8,128)S(1)}, f32[16,256]{1,0:T(8,128)S(1)}, u32[]{:S(2)}, u32[]{:S(2)}) collective-permute-start(f32[16,256]{1,0:T(8,128)S(1)} %fusion), channel_id=1, source_target_pairs={{0,30},{1,31},{2,32},{3,33},{4,34},{5,35},{6,36},{7,37},{8,38},{9,... | collective-permute-start | bytes 49160
  1422.8 23.8 %collective-permute-start.3 = (f32[16,256]{1,0:T(8,128)S(1)}, f32[16,256]{1,0:T(8,128)S(1)}, u32[]{:S(2)}, u32[]{:S(2)}) collective-permute-start(f32[16,256]{1,0:T(8,128)S(1)} %fusion), channel_id=1, source_target_pairs={{0,4},{1,5},{2,6},{3,7},{4,8},{5,9},{6,10},{7,11},{8,12},{9,13},{1... | collective-permute-start | bytes 49160
  1431.5 17.0 %collective-permute-start.30 = (f32[16,256]{1,0:T(8,128)S(1)}, f32[16,256]{1,0:T(8,128)S(1)}, u32[]{:S(2)}, u32[]{:S(2)}) collective-permute-start(f32[16,256]{1,0:T(8,128)S(1)} %fusion), channel_id=1, source_target_pairs={{0,31},{1,32},{2,33},{3,34},{4,35},{5,36},{6,37},{7,38},{8,39},{9,... | collective-permute-start | bytes 49160
  1438.6 11.8 collective-permute-start.31
  1442.7 9.7 collective-permute-start.32
  1444.6 9.7 collective-permute-start.33
  1446.5 9.7 collective-permute-start.34
  1450.4 25.4 %collective-permute-start.36 = (f32[16,256]{1,0:T(8,128)S(1)}, f32[16,256]{1,0:T(8,128)S(1)}, u32[]{:S(2)}, u32[]{:S(2)}) collective-permute-start(f32[16,256]{1,0:T(8,128)S(1)} %fusion), channel_id=1, source_target_pairs={{0,37},{1,38},{2,39},{3,40},{4,41},{5,42},{6,43},{7,44},{8,45},{9,... | collective-permute-start | bytes 49160
  1452.3 30.5 %collective-permute-start.37 = (f32[16,256]{1,0:T(8,128)S(1)}, f32[16,256]{1,0:T(8,128)S(1)}, u32[]{:S(2)}, u32[]{:S(2)}) collective-permute-start(f32[16,256]{1,0:T(8,128)S(1)} %fusion), channel_id=1, source_target_pairs={{0,38},{1,39},{2,40},{3,41},{4,42},{5,43},{6,44},{7,45},{8,46},{9,... | collective-permute-start | bytes 49160
  1454.3 30.5 %collective-permute-start.38 = (f32[16,256]{1,0:T(8,128)S(1)}, f32[16,256]{1,0:T(8,128)S(1)}, u32[]{:S(2)}, u32[]{:S(2)}) collective-permute-start(f32[16,256]{1,0:T(8,128)S(1)} %fusion), channel_id=1, source_target_pairs={{0,39},{1,40},{2,41},{3,42},{4,43},{5,44},{6,45},{7,46},{8,47},{9,... | collective-permute-start | bytes 49160
  1456.2 30.5 %collective-permute-start.39 = (f32[16,256]{1,0:T(8,128)S(1)}, f32[16,256]{1,0:T(8,128)S(1)}, u32[]{:S(2)}, u32[]{:S(2)}) collective-permute-start(f32[16,256]{1,0:T(8,128)S(1)} %fusion), channel_id=1, source_target_pairs={{0,40},{1,41},{2,42},{3,43},{4,44},{5,45},{6,46},{7,47},{8,48},{9,... | collective-permute-start | bytes 49160
  1458.2 30.5 %collective-permute-start.4 = (f32[16,256]{1,0:T(8,128)S(1)}, f32[16,256]{1,0:T(8,128)S(1)}, u32[]{:S(2)}, u32[]{:S(2)}) collective-permute-start(f32[16,256]{1,0:T(8,128)S(1)} %fusion), channel_id=1, source_target_pairs={{0,5},{1,6},{2,7},{3,8},{4,9},{5,10},{6,11},{7,12},{8,13},{9,14},{... | collective-permute-start | bytes 49160
  1475.8 14.7 collective-permute-start.40
  1482.8 10.7 collective-permute-start.41
  1484.8 10.7 collective-permute-start.42
  1486.7 13.0 collective-permute-start.43
  1488.7 13.0 collective-permute-start.44
  1490.6 13.0 collective-permute-start.45
  1493.6 30.9 %collective-permute-start.46 = (f32[16,256]{1,0:T(8,128)S(1)}, f32[16,256]{1,0:T(8,128)S(1)}, u32[]{:S(2)}, u32[]{:S(2)}) collective-permute-start(f32[16,256]{1,0:T(8,128)S(1)} %fusion), channel_id=1, source_target_pairs={{0,47},{1,48},{2,49},{3,50},{4,51},{5,52},{6,53},{7,54},{8,55},{9,... | collective-permute-start | bytes 49160
  1495.5 39.3 %collective-permute-start.47 = (f32[16,256]{1,0:T(8,128)S(1)}, f32[16,256]{1,0:T(8,128)S(1)}, u32[]{:S(2)}, u32[]{:S(2)}) collective-permute-start(f32[16,256]{1,0:T(8,128)S(1)} %fusion), channel_id=1, source_target_pairs={{0,48},{1,49},{2,50},{3,51},{4,52},{5,53},{6,54},{7,55},{8,56},{9,... | collective-permute-start | bytes 49160
  1499.8 36.9 %collective-permute-start.48 = (f32[16,256]{1,0:T(8,128)S(1)}, f32[16,256]{1,0:T(8,128)S(1)}, u32[]{:S(2)}, u32[]{:S(2)}) collective-permute-start(f32[16,256]{1,0:T(8,128)S(1)} %fusion), channel_id=1, source_target_pairs={{0,49},{1,50},{2,51},{3,52},{4,53},{5,54},{6,55},{7,56},{8,57},{9,... | collective-permute-start | bytes 49160
  1501.7 36.9 %collective-permute-start.49 = (f32[16,256]{1,0:T(8,128)S(1)}, f32[16,256]{1,0:T(8,128)S(1)}, u32[]{:S(2)}, u32[]{:S(2)}) collective-permute-start(f32[16,256]{1,0:T(8,128)S(1)} %fusion), channel_id=1, source_target_pairs={{0,50},{1,51},{2,52},{3,53},{4,54},{5,55},{6,56},{7,57},{8,58},{9,... | collective-permute-start | bytes 49160
  1503.6 37.1 %collective-permute-start.5 = (f32[16,256]{1,0:T(8,128)S(1)}, f32[16,256]{1,0:T(8,128)S(1)}, u32[]{:S(2)}, u32[]{:S(2)}) collective-permute-start(f32[16,256]{1,0:T(8,128)S(1)} %fusion), channel_id=1, source_target_pairs={{0,6},{1,7},{2,8},{3,9},{4,10},{5,11},{6,12},{7,13},{8,14},{9,15},... | collective-permute-start | bytes 49160
  1524.4 18.2 %collective-permute-start.50 = (f32[16,256]{1,0:T(8,128)S(1)}, f32[16,256]{1,0:T(8,128)S(1)}, u32[]{:S(2)}, u32[]{:S(2)}) collective-permute-start(f32[16,256]{1,0:T(8,128)S(1)} %fusion), channel_id=1, source_target_pairs={{0,51},{1,52},{2,53},{3,54},{4,55},{5,56},{6,57},{7,58},{8,59},{9,... | collective-permute-start | bytes 49160
  1534.8 9.9 collective-permute-start.51
  1536.7 9.9 collective-permute-start.52
  1538.6 9.9 collective-permute-start.53
  1544.6 21.1 %collective-permute-start.56 = (f32[16,256]{1,0:T(8,128)S(1)}, f32[16,256]{1,0:T(8,128)S(1)}, u32[]{:S(2)}, u32[]{:S(2)}) collective-permute-start(f32[16,256]{1,0:T(8,128)S(1)} %fusion), channel_id=1, source_target_pairs={{0,57},{1,58},{2,59},{3,60},{4,61},{5,62},{6,63},{7,64},{8,65},{9,... | collective-permute-start | bytes 49160
  1546.6 27.1 %collective-permute-start.57 = (f32[16,256]{1,0:T(8,128)S(1)}, f32[16,256]{1,0:T(8,128)S(1)}, u32[]{:S(2)}, u32[]{:S(2)}) collective-permute-start(f32[16,256]{1,0:T(8,128)S(1)} %fusion), channel_id=1, source_target_pairs={{0,58},{1,59},{2,60},{3,61},{4,62},{5,63},{6,64},{7,65},{8,66},{9,... | collective-permute-start | bytes 49160
  1548.5 27.1 %collective-permute-start.58 = (f32[16,256]{1,0:T(8,128)S(1)}, f32[16,256]{1,0:T(8,128)S(1)}, u32[]{:S(2)}, u32[]{:S(2)}) collective-permute-start(f32[16,256]{1,0:T(8,128)S(1)} %fusion), channel_id=1, source_target_pairs={{0,59},{1,60},{2,61},{3,62},{4,63},{5,64},{6,65},{7,66},{8,67},{9,... | collective-permute-start | bytes 49160
  1550.5 27.1 %collective-permute-start.59 = (f32[16,256]{1,0:T(8,128)S(1)}, f32[16,256]{1,0:T(8,128)S(1)}, u32[]{:S(2)}, u32[]{:S(2)}) collective-permute-start(f32[16,256]{1,0:T(8,128)S(1)} %fusion), channel_id=1, source_target_pairs={{0,60},{1,61},{2,62},{3,63},{4,64},{5,65},{6,66},{7,67},{8,68},{9,... | collective-permute-start | bytes 49160
  1552.4 34.9 %collective-permute-start.6 = (f32[16,256]{1,0:T(8,128)S(1)}, f32[16,256]{1,0:T(8,128)S(1)}, u32[]{:S(2)}, u32[]{:S(2)}) collective-permute-start(f32[16,256]{1,0:T(8,128)S(1)} %fusion), channel_id=1, source_target_pairs={{0,7},{1,8},{2,9},{3,10},{4,11},{5,12},{6,13},{7,14},{8,15},{9,16}... | collective-permute-start | bytes 49160
  1565.7 34.8 %collective-permute-start.60 = (f32[16,256]{1,0:T(8,128)S(1)}, f32[16,256]{1,0:T(8,128)S(1)}, u32[]{:S(2)}, u32[]{:S(2)}) collective-permute-start(f32[16,256]{1,0:T(8,128)S(1)} %fusion), channel_id=1, source_target_pairs={{0,61},{1,62},{2,63},{3,64},{4,65},{5,66},{6,67},{7,68},{8,69},{9,... | collective-permute-start | bytes 49160
  1573.7 39.9 %collective-permute-start.61 = (f32[16,256]{1,0:T(8,128)S(1)}, f32[16,256]{1,0:T(8,128)S(1)}, u32[]{:S(2)}, u32[]{:S(2)}) collective-permute-start(f32[16,256]{1,0:T(8,128)S(1)} %fusion), channel_id=1, source_target_pairs={{0,62},{1,63},{2,64},{3,65},{4,66},{5,67},{6,68},{7,69},{8,70},{9,... | collective-permute-start | bytes 49160
  1575.6 38.0 %collective-permute-start.62 = (f32[16,256]{1,0:T(8,128)S(1)}, f32[16,256]{1,0:T(8,128)S(1)}, u32[]{:S(2)}, u32[]{:S(2)}) collective-permute-start(f32[16,256]{1,0:T(8,128)S(1)} %fusion), channel_id=1, source_target_pairs={{0,63},{1,64},{2,65},{3,66},{4,67},{5,68},{6,69},{7,70},{8,71},{9,... | collective-permute-start | bytes 49160
  1577.6 36.1 %collective-permute-start.7 = (f32[16,256]{1,0:T(8,128)S(1)}, f32[16,256]{1,0:T(8,128)S(1)}, u32[]{:S(2)}, u32[]{:S(2)}) collective-permute-start(f32[16,256]{1,0:T(8,128)S(1)} %fusion), channel_id=1, source_target_pairs={{0,8},{1,9},{2,10},{3,11},{4,12},{5,13},{6,14},{7,15},{8,16},{9,17... | collective-permute-start | bytes 49160
  1587.3 26.3 %collective-permute-start.8 = (f32[16,256]{1,0:T(8,128)S(1)}, f32[16,256]{1,0:T(8,128)S(1)}, u32[]{:S(2)}, u32[]{:S(2)}) collective-permute-start(f32[16,256]{1,0:T(8,128)S(1)} %fusion), channel_id=1, source_target_pairs={{0,9},{1,10},{2,11},{3,12},{4,13},{5,14},{6,15},{7,16},{8,17},{9,1... | collective-permute-start | bytes 49160
  1600.5 23.3 %collective-permute-start.9 = (f32[16,256]{1,0:T(8,128)S(1)}, f32[16,256]{1,0:T(8,128)S(1)}, u32[]{:S(2)}, u32[]{:S(2)}) collective-permute-start(f32[16,256]{1,0:T(8,128)S(1)} %fusion), channel_id=1, source_target_pairs={{0,10},{1,11},{2,12},{3,13},{4,14},{5,15},{6,16},{7,17},{8,18},{9,... | collective-permute-start | bytes 49160
  (25 other events, 99.6 us)
Sparse Core Ops, SparseCore 0:
  9.8 124.8 all-gather.1
  469.4 280.4 all-reduce.38
